TPU v7x, 128 devices: a whole 4x4x4 slice. The times are simulated.
128 devices in a mesh: src: 8 (over z_hi, y), obs: 16 (over x, z_lo, core).
Axes of the slice: x: 4, y: 4, z: 4 (z_hi: 2, z_lo: 2; z = z_hi * 2 + z_lo), core: 2. Of those that a mesh axis runs over, the one named last changes fastest.
Arguments:
- tiles: bfloat16 [8, 16, 512, 128, 128], P('src', 'obs'), may hold values from -0.25 to 0.25
- tile_index: int32 [8, 16, 3, 512], P('src', 'obs'), may hold values from 0 to 1023, as said below
- tile_count: int32 [8, 16], P('src', 'obs'), may hold values from 64 to 512, as said below
- history: bfloat16 [16, 4, 1048576], P(None, None, ('src', 'obs')), may hold values from -6 to 6
- incident: float32 [2, 4, 1048576], P(None, None, ('src', 'obs')), may hold values from -6 to 6
- near_inverse: bfloat16 [8192, 128, 128], P(('src', 'obs')), may hold values from -0.5 to 0.5
Outputs:
- densities: bfloat16 [2, 4, 1048576], P(None, None, ('src', 'obs'))
Inputs may be any that keep to these rules, and one draw needn't show every extreme that they name: `tile_index`: row 0 is an observer block among the 512 of a device, row 1 a source block among its 1024, row 2 a delay slot below 16; slots at or past the device's count are padding; a tile may repeat. `tile_count`: live tile slots of each device, the first ones of its list.
All inputs are finite; a program needn't handle non-finite values.
Results may differ from a plain program's by a relative error of at most 0.005.
Values may be sent and summed in bfloat16 or wider, within the bound.
A program may use at most 128 MiB of HBM per device.

v0:
```python
import jax
import jax.numpy as jnp
from jax import lax
from jax.sharding import PartitionSpec as P


def on_device(tiles, tile_index, tile_count, history, incident, near_inverse):
    tile_rows = tiles.reshape(tiles.shape[2], tiles.shape[3], tiles.shape[4])
    index_rows = tile_index.reshape(3, tile_index.shape[3])
    live_count = tile_count.reshape(())
    blocks_own = near_inverse.shape[0]
    tile_width = near_inverse.shape[1]
    coefficients = history.shape[1]
    slot_count = history.shape[0]
    observer_owned = blocks_own * lax.axis_size("src")
    total_tiles = tile_rows.shape[0]
    group_size = min(64, total_tiles)
    loop_turns = total_tiles // group_size

    def accumulate(chooser):

        def one_group(turn_index, partial_value):
            start = turn_index * group_size
            tile_part = lax.dynamic_slice_in_dim(tile_rows, start, group_size, 0)
            index_part = lax.dynamic_slice_in_dim(index_rows, start, group_size, 1)
            operand = chooser(index_part, start)
            products = jnp.einsum(
                "gck,gki->cgi", operand, tile_part, preferred_element_type=jnp.float32
            )
            alive_mask = start + jnp.arange(group_size, dtype=jnp.int32) < live_count
            products = jnp.where(alive_mask[None, :, None], products, 0.0)
            return partial_value.at[:, index_part[0]].add(products)

        initial = jnp.zeros((coefficients, observer_owned, tile_width), jnp.float32)
        return lax.fori_loop(0, loop_turns, one_group, initial)

    def settle(partial_value, drive):
        summed = lax.psum(partial_value, "src")
        own_share = lax.dynamic_slice_in_dim(
            summed, lax.axis_index("src") * blocks_own, blocks_own, 1
        )
        right_side = (drive - own_share.reshape(coefficients, blocks_own * tile_width)).astype(
            jnp.bfloat16
        )
        right_side = right_side.reshape(coefficients, blocks_own, tile_width)
        solved = jnp.einsum(
            "cbk,bki->cbi", right_side, near_inverse, preferred_element_type=jnp.float32
        )
        return solved.reshape(coefficients, blocks_own * tile_width).astype(jnp.bfloat16)

    gathered = lax.all_gather(history, "obs", axis=2, tiled=True)
    history_src = gathered.reshape(slot_count, coefficients, -1, tile_width)

    def chooser_first(index_part, start):
        return history_src[index_part[2], :, index_part[1]]

    first_new = settle(accumulate(chooser_first), incident[0])
    newest_src = lax.all_gather(first_new, "obs", axis=1, tiled=True).reshape(
        coefficients, -1, tile_width
    )

    def chooser_second(index_part, start):
        source = index_part[1]
        delay_slot = index_part[2]
        older = history_src[jnp.maximum(delay_slot - 1, 0), :, source]
        newer = jnp.swapaxes(newest_src[:, source], 0, 1)
        return jnp.where((delay_slot == 0)[:, None, None], newer, older)

    second_new = settle(accumulate(chooser_second), incident[1])
    return jnp.stack([first_new, second_new])


def solution(mesh):
    in_specs = (
        P("src", "obs", None, None, None),
        P("src", "obs", None, None),
        P("src", "obs"),
        P(None, None, ("src", "obs")),
        P(None, None, ("src", "obs")),
        P(("src", "obs"), None, None),
    )
    out_specs = P(None, None, ("src", "obs"))
    return jax.shard_map(
        on_device, mesh=mesh, in_specs=in_specs, out_specs=out_specs, check_vma=False
    )
```

profile of v0, /device:TPU:0, one launch (start us, length us, event | category | flops | bytes accessed | tf_op | source)
XLA Modules:
  0.0 536.3 jit_solution(3474233912254696265)
XLA Ops:
  8.0 95.1 %all-gather.3.cloned.1.call-done = bf16[16,4,131072]{2,1,0:T(4,128)(2,1)} async-done(((bf16[16,4,8192]{2,1,0:T(4,128)(2,1)}), bf16[16,4,131072]{2,1,0:T(4,128)(2,1)}) %all-gather.3.cloned.1.call-update) | async-done | bytes 16777232 | tf_op jit(solution)/shard_map/all_gather | solution.py:51
  103.3 98.3 %while.28 = (s32[]{:T(128)}, f32[4,512,128]{2,0,1:T(4,128)S(1)}, s32[3,512]{1,0:T(4,128)S(1)}, s32[]{:T(128)}, bf16[512,128,128]{2,1,0:T(8,128)(2,1)}, /*index=5...) while((s32[]{:T(128)}, f32[4,512,128]{2,0,1:T(4,128)S(1)}, ...), condition=%wide.region_2.3_spmd, body=%wide.region_0.2_spmd.sunk | while | flops 8455174 | bytes 2821923 | solution.py:35
  104.0 6.5 %gather_fusion = bf16[64,4,128]{2,1,0:T(4,128)(2,1)S(1)} fusion(bf16[16,4,1024,128]{3,1,2,0:T(4,128)(2,1)} %get-tuple-element.438, s32[64]{0:T(128)S(1)} %get-tuple-element.402), kind=kCustom, calls=%fused_computation.clone.1 | custom fusion | bytes 131584 | tf_op jit(solution)/shard_map/while/body/eval_jaxpr/gather | solution.py:55
  112.8 2.7 scatter_fusion
  116.3 6.5 %gather_fusion = bf16[64,4,128]{2,1,0:T(4,128)(2,1)S(1)} fusion(bf16[16,4,1024,128]{3,1,2,0:T(4,128)(2,1)} %get-tuple-element.438, s32[64]{0:T(128)S(1)} %get-tuple-element.402), kind=kCustom, calls=%fused_computation.clone.1 | custom fusion | bytes 131584 | tf_op jit(solution)/shard_map/while/body/eval_jaxpr/gather | solution.py:55
  125.1 2.7 scatter_fusion
  128.6 6.5 %gather_fusion = bf16[64,4,128]{2,1,0:T(4,128)(2,1)S(1)} fusion(bf16[16,4,1024,128]{3,1,2,0:T(4,128)(2,1)} %get-tuple-element.438, s32[64]{0:T(128)S(1)} %get-tuple-element.402), kind=kCustom, calls=%fused_computation.clone.1 | custom fusion | bytes 131584 | tf_op jit(solution)/shard_map/while/body/eval_jaxpr/gather | solution.py:55
  137.4 2.7 scatter_fusion
  140.9 6.5 %gather_fusion = bf16[64,4,128]{2,1,0:T(4,128)(2,1)S(1)} fusion(bf16[16,4,1024,128]{3,1,2,0:T(4,128)(2,1)} %get-tuple-element.438, s32[64]{0:T(128)S(1)} %get-tuple-element.402), kind=kCustom, calls=%fused_computation.clone.1 | custom fusion | bytes 131584 | tf_op jit(solution)/shard_map/while/body/eval_jaxpr/gather | solution.py:55
  149.7 2.7 scatter_fusion
  153.2 6.5 %gather_fusion = bf16[64,4,128]{2,1,0:T(4,128)(2,1)S(1)} fusion(bf16[16,4,1024,128]{3,1,2,0:T(4,128)(2,1)} %get-tuple-element.438, s32[64]{0:T(128)S(1)} %get-tuple-element.402), kind=kCustom, calls=%fused_computation.clone.1 | custom fusion | bytes 131584 | tf_op jit(solution)/shard_map/while/body/eval_jaxpr/gather | solution.py:55
  162.0 2.7 scatter_fusion
  165.5 6.5 %gather_fusion = bf16[64,4,128]{2,1,0:T(4,128)(2,1)S(1)} fusion(bf16[16,4,1024,128]{3,1,2,0:T(4,128)(2,1)} %get-tuple-element.438, s32[64]{0:T(128)S(1)} %get-tuple-element.402), kind=kCustom, calls=%fused_computation.clone.1 | custom fusion | bytes 131584 | tf_op jit(solution)/shard_map/while/body/eval_jaxpr/gather | solution.py:55
  174.3 2.7 scatter_fusion
  177.8 6.5 %gather_fusion = bf16[64,4,128]{2,1,0:T(4,128)(2,1)S(1)} fusion(bf16[16,4,1024,128]{3,1,2,0:T(4,128)(2,1)} %get-tuple-element.438, s32[64]{0:T(128)S(1)} %get-tuple-element.402), kind=kCustom, calls=%fused_computation.clone.1 | custom fusion | bytes 131584 | tf_op jit(solution)/shard_map/while/body/eval_jaxpr/gather | solution.py:55
  186.6 2.7 scatter_fusion
  190.1 6.5 %gather_fusion = bf16[64,4,128]{2,1,0:T(4,128)(2,1)S(1)} fusion(bf16[16,4,1024,128]{3,1,2,0:T(4,128)(2,1)} %get-tuple-element.438, s32[64]{0:T(128)S(1)} %get-tuple-element.402), kind=kCustom, calls=%fused_computation.clone.1 | custom fusion | bytes 131584 | tf_op jit(solution)/shard_map/while/body/eval_jaxpr/gather | solution.py:55
  198.8 2.7 scatter_fusion
  202.7 88.8 %all-reduce.3.cloned.1.call-done = f32[4,512,128]{2,0,1:T(4,128)} async-done(((f32[4,512,128]{2,0,1:T(4,128)}), f32[4,512,128]{2,0,1:T(4,128)}) %all-reduce.3.cloned.1.call-update) | async-done | bytes 1048592 | tf_op jit(solution)/shard_map/psum | solution.py:38
  293.9 30.2 %all-gather.5.cloned.1.call-done = bf16[4,131072]{1,0:T(4,128)(2,1)} async-done(((bf16[4,8192]{1,0:T(4,128)(2,1)}), bf16[4,131072]{1,0:T(4,128)(2,1)}) %all-gather.5.cloned.1.call-update) | async-done | bytes 1048592 | tf_op jit(solution)/shard_map/all_gather | solution.py:58
  324.2 114.0 %while.29 = (s32[]{:T(128)}, f32[4,512,128]{2,0,1:T(4,128)S(1)}, s32[3,512]{1,0:T(4,128)S(1)}, s32[]{:T(128)}, bf16[512,128,128]{2,1,0:T(8,128)(2,1)}, /*index=5...) while((s32[]{:T(128)}, f32[4,512,128]{2,0,1:T(4,128)S(1)}, ...), condition=%wide.region_6.7_spmd, body=%wide.region_4.6_spmd.sunk | while | flops 8488966 | bytes 3023787 | solution.py:35
  326.9 6.5 %gather_fusion.2 = bf16[64,4,128]{2,1,0:T(4,128)(2,1)S(1)} fusion(bf16[16,4,1024,128]{3,1,2,0:T(4,128)(2,1)} %get-tuple-element.471, s32[64]{0:T(128)S(1)} %get-tuple-element.412), kind=kCustom, calls=%fused_computation.2.clone.1 | custom fusion | bytes 131584 | tf_op jit(solution)/shard_map/while/body/eval_jaxpr/gather | solution.py:65
  341.1 6.5 %gather_fusion.2 = bf16[64,4,128]{2,1,0:T(4,128)(2,1)S(1)} fusion(bf16[16,4,1024,128]{3,1,2,0:T(4,128)(2,1)} %get-tuple-element.471, s32[64]{0:T(128)S(1)} %get-tuple-element.412), kind=kCustom, calls=%fused_computation.2.clone.1 | custom fusion | bytes 131584 | tf_op jit(solution)/shard_map/while/body/eval_jaxpr/gather | solution.py:65
  350.0 2.7 scatter_fusion.1
  355.4 6.5 %gather_fusion.2 = bf16[64,4,128]{2,1,0:T(4,128)(2,1)S(1)} fusion(bf16[16,4,1024,128]{3,1,2,0:T(4,128)(2,1)} %get-tuple-element.471, s32[64]{0:T(128)S(1)} %get-tuple-element.412), kind=kCustom, calls=%fused_computation.2.clone.1 | custom fusion | bytes 131584 | tf_op jit(solution)/shard_map/while/body/eval_jaxpr/gather | solution.py:65
  364.2 2.7 scatter_fusion.1
  369.7 6.5 %gather_fusion.2 = bf16[64,4,128]{2,1,0:T(4,128)(2,1)S(1)} fusion(bf16[16,4,1024,128]{3,1,2,0:T(4,128)(2,1)} %get-tuple-element.471, s32[64]{0:T(128)S(1)} %get-tuple-element.412), kind=kCustom, calls=%fused_computation.2.clone.1 | custom fusion | bytes 131584 | tf_op jit(solution)/shard_map/while/body/eval_jaxpr/gather | solution.py:65
  383.9 6.5 %gather_fusion.2 = bf16[64,4,128]{2,1,0:T(4,128)(2,1)S(1)} fusion(bf16[16,4,1024,128]{3,1,2,0:T(4,128)(2,1)} %get-tuple-element.471, s32[64]{0:T(128)S(1)} %get-tuple-element.412), kind=kCustom, calls=%fused_computation.2.clone.1 | custom fusion | bytes 131584 | tf_op jit(solution)/shard_map/while/body/eval_jaxpr/gather | solution.py:65
  398.2 6.5 %gather_fusion.2 = bf16[64,4,128]{2,1,0:T(4,128)(2,1)S(1)} fusion(bf16[16,4,1024,128]{3,1,2,0:T(4,128)(2,1)} %get-tuple-element.471, s32[64]{0:T(128)S(1)} %get-tuple-element.412), kind=kCustom, calls=%fused_computation.2.clone.1 | custom fusion | bytes 131584 | tf_op jit(solution)/shard_map/while/body/eval_jaxpr/gather | solution.py:65
  412.4 6.5 %gather_fusion.2 = bf16[64,4,128]{2,1,0:T(4,128)(2,1)S(1)} fusion(bf16[16,4,1024,128]{3,1,2,0:T(4,128)(2,1)} %get-tuple-element.471, s32[64]{0:T(128)S(1)} %get-tuple-element.412), kind=kCustom, calls=%fused_computation.2.clone.1 | custom fusion | bytes 131584 | tf_op jit(solution)/shard_map/while/body/eval_jaxpr/gather | solution.py:65
  426.7 6.5 %gather_fusion.2 = bf16[64,4,128]{2,1,0:T(4,128)(2,1)S(1)} fusion(bf16[16,4,1024,128]{3,1,2,0:T(4,128)(2,1)} %get-tuple-element.471, s32[64]{0:T(128)S(1)} %get-tuple-element.412), kind=kCustom, calls=%fused_computation.2.clone.1 | custom fusion | bytes 131584 | tf_op jit(solution)/shard_map/while/body/eval_jaxpr/gather | solution.py:65
  439.3 88.1 %all-reduce.5.cloned.1.call-done = f32[4,512,128]{2,0,1:T(4,128)} async-done(((f32[4,512,128]{2,0,1:T(4,128)}), f32[4,512,128]{2,0,1:T(4,128)}) %all-reduce.5.cloned.1.call-update) | async-done | bytes 1048592 | tf_op jit(solution)/shard_map/psum | solution.py:38
  (116 shorter events, 88.3 us)
Async XLA Ops:
  6.5 285.0 %copy-start = (bf16[64,128,128]{2,1,0:T(8,128)(2,1)S(1)}, bf16[64,128,128]{2,1,0:T(8,128)(2,1)}, u32[]{:S(2)}) copy-start(bf16[64,128,128]{2,1,0:T(8,128)(2,1)} %param.15) | copy-start | bytes 6291460
  6.5 96.6 %all-gather.3.cloned.1.call-start = ((), (), s32[]{:S(2)}) async-start(), calls=%async_computation | async-start | bytes 17825792 | tf_op jit(solution)/shard_map/all_gather | solution.py:51
  7.3 284.3 %all-reduce.3.cloned.1.call-start = ((), (), s32[]{:S(2)}) async-start(), calls=%async_computation.1 | async-start | bytes 2097152 | tf_op jit(solution)/shard_map/psum | solution.py:38
  201.6 1.0 copy-start.2
  202.7 121.4 %all-gather.5.cloned.1.call-start = ((), (), s32[]{:S(2)}) async-start(), calls=%async_computation.2 | async-start | bytes 1114112 | tf_op jit(solution)/shard_map/all_gather | solution.py:58
  293.8 233.6 %all-reduce.5.cloned.1.call-start = ((), (), s32[]{:S(2)}) async-start(), calls=%async_computation.3 | async-start | bytes 2097152 | tf_op jit(solution)/shard_map/psum | solution.py:38
  438.2 1.0 copy-start.1
  438.3 90.8 %copy-start.3 = (bf16[64,4,128]{2,1,0:T(4,128)(2,1)S(1)}, bf16[64,4,128]{2,1,0:T(4,128)(2,1)}, u32[]{:S(2)}) copy-start(bf16[64,4,128]{2,1,0:T(4,128)(2,1)} %convolution_convert_fusion.1) | copy-start | bytes 196612
Sparse Core Ops, SparseCore 0:
  9.0 94.0 all-gather.2
  202.8 88.7 all-reduce.2
  294.0 30.0 all-gather.4
  439.4 87.9 all-reduce.4
where the time goes:
time: 538 us; the launch traced here: 536 us
  waiting for transfers between devices  303 us (56%)
  local copies, waits for them, and re-layouts  124 us (23%)
  other arithmetic  55.4 us (10%)
  matrix products  40.1 us (7%)
  between operations  13.2 us (2%)
    psum x2, waiting for transfers between devices, settle(): summed = lax.psum(partial_value, 'src')  177 us
    all_gather x1, waiting for transfers between devices, on_device(): gathered = lax.all_gather(history, 'obs', axis=2, tiled=True)  95.1 us
    gather x8, local copies, waits for them, and re-layouts, chooser_second(): older = history_src[jnp.maximum(delay_slot - 1, 0), :, source]  52.3 us
    gather x8, local copies, waits for them, and re-layouts, chooser_first(): return history_src[index_part[2], :, index_part[1]]  52.2 us
    scatter-add x16, other arithmetic, one_group(): return partial_value.at[:, index_part[0]].add(products)  43.9 us
    dot_general x16, matrix products, one_group(): jnp.einsum('gck,gki->cgi', operand, tile_part, preferred_element_type=jnp...  36.3 us
    all_gather x1, waiting for transfers between devices, on_device(): lax.all_gather(first_new, 'obs', axis=1, tiled=True)  30.2 us
    gather x8, local copies, waits for them, and re-layouts, chooser_second(): newer = jnp.swapaxes(newest_src[:, source], 0, 1)  15 us
  transfers between devices with their start and end apart: 4, of which 4 were waited for; matrix products, arithmetic and copies ran while one was open for 0% of the time, Pallas kernels for 0%

commit v1 on v0

--- a/solution.py
+++ b/solution.py
@@ -2,6 +2,7 @@
 import jax.numpy as jnp
 from jax import lax
 from jax.sharding import PartitionSpec as P
+from jax.lax import all_gather
 
 
 def on_device(tiles, tile_index, tile_count, history, incident, near_inverse):
@@ -35,7 +36,7 @@
         return lax.fori_loop(0, loop_turns, one_group, initial)
 
     def settle(partial_value, drive):
-        summed = lax.psum(partial_value, "src")
+        summed = all_gather(partial_value, "src").sum(axis=0)
         own_share = lax.dynamic_slice_in_dim(
             summed, lax.axis_index("src") * blocks_own, blocks_own, 1
         )

time: 538 us -> 585 us (1.087)
  waiting for transfers between devices: 303 us -> 343 us
  other arithmetic: 55.4 us -> 63.2 us
    all_gather x0 -> x2, waiting for transfers between devices: none -> 217 us  [settle(): summed = all_gather(partial_value, 'src').sum(axis=0)]
    psum x2 -> x0, waiting for transfers between devices: 177 us -> none  [settle(): summed = lax.psum(partial_value, 'src')]
    reduce_sum x0 -> x2, other arithmetic: none -> 7.82 us  [settle(): summed = all_gather(partial_value, 'src').sum(axis=0)]
where the time goes in v1:
time: 585 us; the launch traced here: 583 us
  waiting for transfers between devices  343 us (59%)
  local copies, waits for them, and re-layouts  125 us (21%)
  other arithmetic  63.2 us (11%)
  matrix products  38.3 us (7%)
  between operations  13.2 us (2%)
    all_gather x2, waiting for transfers between devices, settle(): summed = all_gather(partial_value, 'src').sum(axis=0)  217 us
    all_gather x1, waiting for transfers between devices, on_device(): gathered = lax.all_gather(history, 'obs', axis=2, tiled=True)  95.1 us
    gather x8, local copies, waits for them, and re-layouts, chooser_second(): older = history_src[jnp.maximum(delay_slot - 1, 0), :, source]  52.3 us
    gather x8, local copies, waits for them, and re-layouts, chooser_first(): return history_src[index_part[2], :, index_part[1]]  52.2 us
    scatter-add x16, other arithmetic, one_group(): return partial_value.at[:, index_part[0]].add(products)  43.9 us
    dot_general x16, matrix products, one_group(): jnp.einsum('gck,gki->cgi', operand, tile_part, preferred_element_type=jnp...  36.4 us
    all_gather x1, waiting for transfers between devices, on_device(): lax.all_gather(first_new, 'obs', axis=1, tiled=True)  29.9 us
    gather x8, local copies, waits for them, and re-layouts, chooser_second(): newer = jnp.swapaxes(newest_src[:, source], 0, 1)  15 us
  transfers between devices with their start and end apart: 4, of which 4 were waited for; matrix products, arithmetic and copies ran while one was open for 0% of the time, Pallas kernels for 0%

profile of v1, /device:TPU:0, one launch (start us, length us, event | category | flops | bytes accessed | tf_op | source)
XLA Modules:
  0.0 583.2 jit_solution(15191931974205112584)
XLA Ops:
  8.0 95.1 %all-gather.7.cloned.1.call-done = bf16[16,4,131072]{2,1,0:T(4,128)(2,1)} async-done(((bf16[16,4,8192]{2,1,0:T(4,128)(2,1)}), bf16[16,4,131072]{2,1,0:T(4,128)(2,1)}) %all-gather.7.cloned.1.call-update) | async-done | bytes 16777232 | tf_op jit(solution)/shard_map/all_gather | solution.py:52
  103.3 98.4 %while.28 = (s32[]{:T(128)}, f32[4,512,128]{2,0,1:T(4,128)S(1)}, s32[3,512]{1,0:T(4,128)S(1)}, s32[]{:T(128)}, bf16[512,128,128]{2,1,0:T(8,128)(2,1)}, /*index=5...) while((s32[]{:T(128)}, f32[4,512,128]{2,0,1:T(4,128)S(1)}, ...), condition=%wide.region_2.3_spmd, body=%wide.region_0.2_spmd.sunk | while | flops 8455174 | bytes 2821923 | solution.py:36
  103.4 6.5 %gather_fusion = bf16[64,4,128]{2,1,0:T(4,128)(2,1)S(1)} fusion(bf16[16,4,1024,128]{3,1,2,0:T(4,128)(2,1)} %get-tuple-element.440, s32[64]{0:T(128)S(1)} %get-tuple-element.404), kind=kCustom, calls=%fused_computation.clone.1 | custom fusion | bytes 131584 | tf_op jit(solution)/shard_map/while/body/eval_jaxpr/gather | solution.py:56
  112.8 2.7 scatter_fusion
  115.7 6.5 %gather_fusion = bf16[64,4,128]{2,1,0:T(4,128)(2,1)S(1)} fusion(bf16[16,4,1024,128]{3,1,2,0:T(4,128)(2,1)} %get-tuple-element.440, s32[64]{0:T(128)S(1)} %get-tuple-element.404), kind=kCustom, calls=%fused_computation.clone.1 | custom fusion | bytes 131584 | tf_op jit(solution)/shard_map/while/body/eval_jaxpr/gather | solution.py:56
  125.1 2.7 scatter_fusion
  128.0 6.5 %gather_fusion = bf16[64,4,128]{2,1,0:T(4,128)(2,1)S(1)} fusion(bf16[16,4,1024,128]{3,1,2,0:T(4,128)(2,1)} %get-tuple-element.440, s32[64]{0:T(128)S(1)} %get-tuple-element.404), kind=kCustom, calls=%fused_computation.clone.1 | custom fusion | bytes 131584 | tf_op jit(solution)/shard_map/while/body/eval_jaxpr/gather | solution.py:56
  137.4 2.7 scatter_fusion
  140.3 6.5 %gather_fusion = bf16[64,4,128]{2,1,0:T(4,128)(2,1)S(1)} fusion(bf16[16,4,1024,128]{3,1,2,0:T(4,128)(2,1)} %get-tuple-element.440, s32[64]{0:T(128)S(1)} %get-tuple-element.404), kind=kCustom, calls=%fused_computation.clone.1 | custom fusion | bytes 131584 | tf_op jit(solution)/shard_map/while/body/eval_jaxpr/gather | solution.py:56
  149.7 2.7 scatter_fusion
  152.5 6.5 %gather_fusion = bf16[64,4,128]{2,1,0:T(4,128)(2,1)S(1)} fusion(bf16[16,4,1024,128]{3,1,2,0:T(4,128)(2,1)} %get-tuple-element.440, s32[64]{0:T(128)S(1)} %get-tuple-element.404), kind=kCustom, calls=%fused_computation.clone.1 | custom fusion | bytes 131584 | tf_op jit(solution)/shard_map/while/body/eval_jaxpr/gather | solution.py:56
  162.0 2.7 scatter_fusion
  164.8 6.5 %gather_fusion = bf16[64,4,128]{2,1,0:T(4,128)(2,1)S(1)} fusion(bf16[16,4,1024,128]{3,1,2,0:T(4,128)(2,1)} %get-tuple-element.440, s32[64]{0:T(128)S(1)} %get-tuple-element.404), kind=kCustom, calls=%fused_computation.clone.1 | custom fusion | bytes 131584 | tf_op jit(solution)/shard_map/while/body/eval_jaxpr/gather | solution.py:56
  177.1 6.5 %gather_fusion = bf16[64,4,128]{2,1,0:T(4,128)(2,1)S(1)} fusion(bf16[16,4,1024,128]{3,1,2,0:T(4,128)(2,1)} %get-tuple-element.440, s32[64]{0:T(128)S(1)} %get-tuple-element.404), kind=kCustom, calls=%fused_computation.clone.1 | custom fusion | bytes 131584 | tf_op jit(solution)/shard_map/while/body/eval_jaxpr/gather | solution.py:56
  186.6 2.7 scatter_fusion
  189.4 6.5 %gather_fusion = bf16[64,4,128]{2,1,0:T(4,128)(2,1)S(1)} fusion(bf16[16,4,1024,128]{3,1,2,0:T(4,128)(2,1)} %get-tuple-element.440, s32[64]{0:T(128)S(1)} %get-tuple-element.404), kind=kCustom, calls=%fused_computation.clone.1 | custom fusion | bytes 131584 | tf_op jit(solution)/shard_map/while/body/eval_jaxpr/gather | solution.py:56
  203.8 108.3 %all-gather.11.cloned.1.call-done = f32[32,512,128]{2,1,0:T(8,128)} async-done(((f32[4,512,128]{2,1,0:T(8,128)}), f32[32,512,128]{2,1,0:T(8,128)}) %all-gather.11.cloned.1.call-update) | async-done | bytes 8388624 | tf_op jit(solution)/shard_map/all_gather | solution.py:39
  312.1 3.9 reduce_sum.18
  317.4 29.9 %all-gather.9.cloned.1.call-done = bf16[4,131072]{1,0:T(4,128)(2,1)} async-done(((bf16[4,8192]{1,0:T(4,128)(2,1)}), bf16[4,131072]{1,0:T(4,128)(2,1)}) %all-gather.9.cloned.1.call-update) | async-done | bytes 1048592 | tf_op jit(solution)/shard_map/all_gather | solution.py:59
  347.5 114.0 %while.29 = (s32[]{:T(128)}, f32[4,512,128]{2,0,1:T(4,128)S(1)}, s32[3,512]{1,0:T(4,128)S(1)}, s32[]{:T(128)}, bf16[512,128,128]{2,1,0:T(8,128)(2,1)}, /*index=5...) while((s32[]{:T(128)}, f32[4,512,128]{2,0,1:T(4,128)S(1)}, ...), condition=%wide.region_6.7_spmd, body=%wide.region_4.6_spmd.sunk | while | flops 8488966 | bytes 3023787 | solution.py:36
  349.5 6.5 %gather_fusion.2 = bf16[64,4,128]{2,1,0:T(4,128)(2,1)S(1)} fusion(bf16[16,4,1024,128]{3,1,2,0:T(4,128)(2,1)} %get-tuple-element.473, s32[64]{0:T(128)S(1)} %get-tuple-element.414), kind=kCustom, calls=%fused_computation.2.clone.1 | custom fusion | bytes 131584 | tf_op jit(solution)/shard_map/while/body/eval_jaxpr/gather | solution.py:66
  363.8 6.5 %gather_fusion.2 = bf16[64,4,128]{2,1,0:T(4,128)(2,1)S(1)} fusion(bf16[16,4,1024,128]{3,1,2,0:T(4,128)(2,1)} %get-tuple-element.473, s32[64]{0:T(128)S(1)} %get-tuple-element.414), kind=kCustom, calls=%fused_computation.2.clone.1 | custom fusion | bytes 131584 | tf_op jit(solution)/shard_map/while/body/eval_jaxpr/gather | solution.py:66
  378.0 6.5 %gather_fusion.2 = bf16[64,4,128]{2,1,0:T(4,128)(2,1)S(1)} fusion(bf16[16,4,1024,128]{3,1,2,0:T(4,128)(2,1)} %get-tuple-element.473, s32[64]{0:T(128)S(1)} %get-tuple-element.414), kind=kCustom, calls=%fused_computation.2.clone.1 | custom fusion | bytes 131584 | tf_op jit(solution)/shard_map/while/body/eval_jaxpr/gather | solution.py:66
  387.5 2.7 scatter_fusion.1
  392.3 6.5 %gather_fusion.2 = bf16[64,4,128]{2,1,0:T(4,128)(2,1)S(1)} fusion(bf16[16,4,1024,128]{3,1,2,0:T(4,128)(2,1)} %get-tuple-element.473, s32[64]{0:T(128)S(1)} %get-tuple-element.414), kind=kCustom, calls=%fused_computation.2.clone.1 | custom fusion | bytes 131584 | tf_op jit(solution)/shard_map/while/body/eval_jaxpr/gather | solution.py:66
  401.8 2.7 scatter_fusion.1
  406.5 6.5 %gather_fusion.2 = bf16[64,4,128]{2,1,0:T(4,128)(2,1)S(1)} fusion(bf16[16,4,1024,128]{3,1,2,0:T(4,128)(2,1)} %get-tuple-element.473, s32[64]{0:T(128)S(1)} %get-tuple-element.414), kind=kCustom, calls=%fused_computation.2.clone.1 | custom fusion | bytes 131584 | tf_op jit(solution)/shard_map/while/body/eval_jaxpr/gather | solution.py:66
  420.8 6.5 %gather_fusion.2 = bf16[64,4,128]{2,1,0:T(4,128)(2,1)S(1)} fusion(bf16[16,4,1024,128]{3,1,2,0:T(4,128)(2,1)} %get-tuple-element.473, s32[64]{0:T(128)S(1)} %get-tuple-element.414), kind=kCustom, calls=%fused_computation.2.clone.1 | custom fusion | bytes 131584 | tf_op jit(solution)/shard_map/while/body/eval_jaxpr/gather | solution.py:66
  435.0 6.5 %gather_fusion.2 = bf16[64,4,128]{2,1,0:T(4,128)(2,1)S(1)} fusion(bf16[16,4,1024,128]{3,1,2,0:T(4,128)(2,1)} %get-tuple-element.473, s32[64]{0:T(128)S(1)} %get-tuple-element.414), kind=kCustom, calls=%fused_computation.2.clone.1 | custom fusion | bytes 131584 | tf_op jit(solution)/shard_map/while/body/eval_jaxpr/gather | solution.py:66
  449.3 6.5 %gather_fusion.2 = bf16[64,4,128]{2,1,0:T(4,128)(2,1)S(1)} fusion(bf16[16,4,1024,128]{3,1,2,0:T(4,128)(2,1)} %get-tuple-element.473, s32[64]{0:T(128)S(1)} %get-tuple-element.414), kind=kCustom, calls=%fused_computation.2.clone.1 | custom fusion | bytes 131584 | tf_op jit(solution)/shard_map/while/body/eval_jaxpr/gather | solution.py:66
  462.7 108.6 %all-gather.13.cloned.1.call-done = f32[32,512,128]{2,1,0:T(8,128)} async-done(((f32[4,512,128]{2,1,0:T(8,128)}), f32[32,512,128]{2,1,0:T(8,128)}) %all-gather.13.cloned.1.call-update) | async-done | bytes 8388624 | tf_op jit(solution)/shard_map/all_gather | solution.py:39
  571.3 3.9 reduce_sum.19
  (119 shorter events, 93.1 us)
Async XLA Ops:
  6.5 309.5 %copy-start = (bf16[64,128,128]{2,1,0:T(8,128)(2,1)S(1)}, bf16[64,128,128]{2,1,0:T(8,128)(2,1)}, u32[]{:S(2)}) copy-start(bf16[64,128,128]{2,1,0:T(8,128)(2,1)} %param.15) | copy-start | bytes 6291460
  6.5 96.6 %all-gather.7.cloned.1.call-start = ((), (), s32[]{:S(2)}) async-start(), calls=%async_computation | async-start | bytes 17825792 | tf_op jit(solution)/shard_map/all_gather | solution.py:52
  7.3 304.9 %all-gather.11.cloned.1.call-start = ((), (), s32[]{:S(2)}) async-start(), calls=%async_computation.2 | async-start | bytes 9437184 | tf_op jit(solution)/shard_map/all_gather | solution.py:39
  202.8 144.6 %all-gather.9.cloned.1.call-start = ((), (), s32[]{:S(2)}) async-start(), calls=%async_computation.1 | async-start | bytes 1114112 | tf_op jit(solution)/shard_map/all_gather | solution.py:59
  317.4 253.9 %all-gather.13.cloned.1.call-start = ((), (), s32[]{:S(2)}) async-start(), calls=%async_computation.3 | async-start | bytes 9437184 | tf_op jit(solution)/shard_map/all_gather | solution.py:39
  571.3 4.6 copy-start.1
Sparse Core Ops, SparseCore 0:
  9.0 94.0 all-gather.6
  202.9 109.1 all-gather.10
  317.5 29.8 all-gather.8
  462.8 108.4 all-gather.12
